TPU v7x, 32 devices: a whole 2x2x4 slice. The times are simulated.
32 devices in a mesh: sec: 2 (over x), blk: 8 (over z, y), mp: 2 (over core).
Axes of the slice: x: 2, y: 2, z: 4, core: 2. Of those that a mesh axis runs over, the one named last changes fastest.
Arguments:
- image_pooled: bfloat16 [1536, 1536], P('blk', ('sec', 'mp')), may hold values from -4 to 4
- text_pooled: bfloat16 [1536, 2048], P('blk', ('sec', 'mp')), may hold values from -4 to 4
- image_proj: bfloat16 [1536, 1152], P(('sec', 'mp')), may hold values from -0.15625 to 0.15625
- text_proj: bfloat16 [2048, 1152], P(('sec', 'mp')), may hold values from -0.125 to 0.125
- natural_log_multiplier: float32 [1], replicated, may hold values from 1.4 to 2.3
- logit_bias: float32 [1], replicated, may hold values from -2 to -0.5
- match_cluster_labels: int32 [1536], P('blk'), may hold values from 0 to 1535
Outputs:
- pair_loss: float32 [2, 1536], P('sec', 'blk')
- image_grad: bfloat16 [1536, 1536], P('blk', ('sec', 'mp'))
- text_grad: bfloat16 [1536, 2048], P('blk', ('sec', 'mp'))
All inputs are finite; a program needn't handle non-finite values.
Results may differ from a plain program's by a relative error of at most 0.0065.
Values may be sent and summed in bfloat16 or wider, within the bound.
No kernel may reach another device: no remote copies, remote signals or barrier semaphores. Data moves between devices by JAX's collectives and lax.ppermute only.
A program may use at most 128 MiB of HBM per device.

v0:
```python
import jax
import jax.numpy as jnp
from jax import lax
from jax.sharding import PartitionSpec as P


def unit_rows(embedding):
    row_norm = jnp.sqrt(jnp.sum(embedding * embedding, axis=1, keepdims=True) + 1e-06)
    return (embedding / row_norm, row_norm)


def per_device(
    image_pooled,
    text_pooled,
    image_proj,
    text_proj,
    natural_log_multiplier,
    logit_bias,
    match_cluster_labels,
):
    part_image = jnp.dot(image_pooled, image_proj, preferred_element_type=jnp.float32)
    part_text = jnp.dot(text_pooled, text_proj, preferred_element_type=jnp.float32)
    stacked = jnp.stack([part_image, part_text])
    section = lax.axis_index("sec")
    both_sums = lax.psum(stacked, ("sec", "mp"))
    own_emb = lax.dynamic_index_in_dim(both_sums, section, 0, keepdims=False)
    other_emb = lax.dynamic_index_in_dim(both_sums, 1 - section, 0, keepdims=False)
    own_unit, own_norm = unit_rows(own_emb)
    resident_slice = own_unit.astype(jnp.bfloat16)
    other_unit, other_norm = unit_rows(other_emb)
    counterpart_slice = other_unit.astype(jnp.bfloat16)
    sharpness_factor = jnp.exp(natural_log_multiplier[0])
    shift_quantity = logit_bias[0]
    visit_rows = lax.all_gather(counterpart_slice, "blk", axis=0, tiled=True)
    visited_ids = lax.all_gather(match_cluster_labels, "blk", axis=0, tiled=True)
    agreement_scores_matrix = (
        sharpness_factor
        * lax.dot_general(
            resident_slice, visit_rows, (((1,), (1,)), ((), ())), preferred_element_type=jnp.float32
        )
        + shift_quantity
    )
    desired_polarity = jnp.where(
        match_cluster_labels[:, None] == visited_ids[None, :], 1.0, -1.0
    ).astype(jnp.float32)
    row_losses = jnp.sum(jax.nn.softplus(-desired_polarity * agreement_scores_matrix), axis=1)
    penalty_factor = (
        -sharpness_factor
        * desired_polarity
        * jax.nn.sigmoid(-desired_polarity * agreement_scores_matrix)
    ).astype(jnp.bfloat16)
    unit_grad = jnp.dot(penalty_factor, visit_rows, preferred_element_type=jnp.float32)
    unit_grad, row_losses = (unit_grad, row_losses)
    projection = jnp.sum(own_unit * unit_grad, axis=1, keepdims=True)
    own_demb = ((unit_grad - own_unit * projection) / own_norm).astype(jnp.bfloat16)
    both_grads = lax.all_gather(own_demb[None], "sec", axis=0, tiled=True)
    image_grad = lax.dot_general(
        both_grads[0], image_proj, (((1,), (1,)), ((), ())), preferred_element_type=jnp.float32
    ).astype(jnp.bfloat16)
    text_grad = lax.dot_general(
        both_grads[1], text_proj, (((1,), (1,)), ((), ())), preferred_element_type=jnp.float32
    ).astype(jnp.bfloat16)
    return (row_losses[None, :], image_grad, text_grad)


def solution(mesh):
    placed = (
        P("blk", ("sec", "mp")),
        P("blk", ("sec", "mp")),
        P(("sec", "mp"), None),
        P(("sec", "mp"), None),
        P(),
        P(),
        P("blk"),
    )
    return jax.shard_map(
        per_device,
        mesh=mesh,
        in_specs=placed,
        out_specs=(P("sec", "blk"), P("blk", ("sec", "mp")), P("blk", ("sec", "mp"))),
        check_vma=False,
    )
```

profile of v0, /device:TPU:0, one launch (start us, length us, event | category | flops | bytes accessed | tf_op | source)
XLA Modules:
  0.0 155.9 jit_solution(17890607806463199969)
XLA Ops:
  7.2 0.0 copy-start
  7.2 0.0 copy-start.4
  7.2 0.0 copy-start.2
  7.2 0.0 all-reduce.3.cloned.1.call-start
  7.2 1.2 copy-done
  8.4 1.4 convolution_bitcast_fusion
  9.8 0.0 copy-done.4
  9.8 0.0 copy-done.2
  9.8 0.4 convolution_bitcast_fusion.1
  10.2 1.3 pad_maximum_fusion
  11.6 0.0 all-reduce.3.cloned.1.call-update
  11.6 0.0 all-gather.3.cloned.1.call-start
  11.6 48.8 %all-reduce.3.cloned.1.call-done = f32[2,192,1152]{2,1,0:T(8,128)} async-done(((f32[2,192,1152]{2,1,0:T(8,128)}), f32[2,192,1152]{2,1,0:T(8,128)}) %all-reduce.3.cloned.1.call-update) | async-done | bytes 1769488 | tf_op jit(solution)/shard_map/psum | solution.py:25
  60.5 0.0 copy-start.1
  60.5 1.8 %fusion.7 = (f32[192]{0:T(256)S(1)}, f32[192]{0:T(256)S(1)}) fusion(f32[2,192,1152]{2,1,0:T(8,128)} %all-reduce.3.cloned.1.call-done, s32[]{:T(128)S(6)} %select_n.16, s32[]{:T(128)S(6)} %select_n.17), kind=kLoop, calls=%fused_computation.20 | loop fusion | flops 884352 | bytes 1771016 | tf_op jit(solution)/shard_map/reduce_sum | solution.py:8
  62.2 0.0 copy-start.7
  62.3 0.0 copy-start.5
  62.3 0.2 copy-done.1
  62.5 0.9 fusion.6
  63.4 0.0 all-gather.3.cloned.1.call-update
  64.7 0.0 copy-done.7
  64.8 0.6 dynamic-slice
  66.0 0.0 copy-done.5
  66.0 0.3 dynamic-update-slice
  66.3 12.1 %all-reduce = s32[1536]{0:T(1024)S(1)} all-reduce(s32[1536]{0:T(1024)S(1)} %dynamic-update-slice), channel_id=1, replica_groups=mesh['sec'=2,'blk'=8,'mp'=2] {'blk'}, use_global_device_ids=true, to_apply=%add | all-reduce | flops 1536 | bytes 12288
  78.4 50.5 %all-gather.3.cloned.1.call-done = bf16[1536,1152]{1,0:T(8,128)(2,1)} async-done(((bf16[192,1152]{1,0:T(8,128)(2,1)}), bf16[1536,1152]{1,0:T(8,128)(2,1)}) %all-gather.3.cloned.1.call-update) | async-done | bytes 3538960 | tf_op jit(solution)/shard_map/all_gather | solution.py:34
  128.9 0.0 copy-start.6
  128.9 4.7 %fusion.4 = (f32[192]{0:T(256)}, f32[192,1536]{1,0:T(8,128)S(1)}) fusion(f32[]{:T(128)} %bitcast.37, bf16[1536,1152]{1,0:T(8,128)(2,1)} %all-gather.3.cloned.1.call-done, f32[192]{0:T(256)S(1)} %add_sqrt_fusion.1, f32[2,192,1152]{2,1,0:T(8,128)S(1)} %copy-done.1, s32[]{:T(128)S(6)} %select_n.16, f32[]{:T(128)} %bitcast.1, s32[1536]{0:T(1024)S(1)} %all-reduce, ...), kind=kOutput, calls=%fused_computation.11 | convolution fusion | flops 683753280 | bytes 5614348 | tf_op jit(solution)/shard_map/dot_general | solution.py:38
  133.6 0.0 copy-done.6
  133.6 1.1 multiply_reduce_fusion
  134.7 0.2 divide_convert_fusion
  135.0 0.0 copy-start.3
  135.0 11.7 %all-gather = bf16[384,1152]{1,0:T(8,128)(2,1)S(1)} all-gather(bf16[192,1152]{1,0:T(8,128)(2,1)S(1)} %divide_convert_fusion), channel_id=2, replica_groups=mesh['sec'=2,'blk'=8,'mp'=2] {'sec'}, dimensions={0}, use_global_device_ids=true | all-gather | bytes 1327104 | tf_op jit(solution)/shard_map/all_gather | solution.py:56
  146.7 0.0 copy-done.3
  146.7 1.1 convolution_convert_fusion.1
  147.8 1.2 convolution_convert_fusion
  (3 shorter events, 0.0 us)
Async XLA Ops:
  7.2 1.3 copy-start
  7.2 2.6 %copy-start.4 = (bf16[192,384]{1,0:T(8,128)(2,1)S(1)}, bf16[192,384]{1,0:T(8,128)(2,1)}, u32[]{:S(2)}) copy-start(bf16[192,384]{1,0:T(8,128)(2,1)} %param.7) | copy-start | bytes 442372
  7.2 2.6 %copy-start.2 = (bf16[384,1152]{1,0:T(8,128)(2,1)S(1)}, bf16[384,1152]{1,0:T(8,128)(2,1)}, u32[]{:S(2)}) copy-start(bf16[384,1152]{1,0:T(8,128)(2,1)} %param.9) | copy-start | bytes 2654212
  7.2 53.3 %all-reduce.3.cloned.1.call-start = ((), (), s32[]{:S(2)}) async-start(), calls=%async_computation | async-start | bytes 3538944 | tf_op jit(solution)/shard_map/psum | solution.py:25
  11.6 117.3 %all-gather.3.cloned.1.call-start = ((), (), s32[]{:S(2)}) async-start(), calls=%async_computation.1 | async-start | bytes 3981312 | tf_op jit(solution)/shard_map/all_gather | solution.py:34
  60.5 2.0 %copy-start.1 = (f32[2,192,1152]{2,1,0:T(8,128)S(1)}, f32[2,192,1152]{2,1,0:T(8,128)}, u32[]{:S(2)}) copy-start(f32[2,192,1152]{2,1,0:T(8,128)} %all-reduce.3.cloned.1.call-done) | copy-start | bytes 5308420
  62.2 2.5 %copy-start.7 = (u32[32]{0:T(128)S(1)}, u32[32]{0:T(128)}, u32[]{:S(2)}) copy-start(u32[32]{0:T(128)} %constant.31) | copy-start | bytes 388
  62.3 3.8 %copy-start.5 = (s32[192]{0:T(256)S(1)}, s32[192]{0:T(256)}, u32[]{:S(2)}) copy-start(s32[192]{0:T(256)} %param.13) | copy-start | bytes 2308
  128.9 4.7 %copy-start.6 = (bf16[1536,1152]{1,0:T(8,128)(2,1)S(1)}, bf16[1536,1152]{1,0:T(8,128)(2,1)}, u32[]{:S(2)}) copy-start(bf16[1536,1152]{1,0:T(8,128)(2,1)} %all-gather.3.cloned.1.call-done) | copy-start | bytes 10616836
  135.0 11.8 %copy-start.3 = (bf16[384,1152]{1,0:T(8,128)(2,1)S(1)}, bf16[384,1152]{1,0:T(8,128)(2,1)}, u32[]{:S(2)}) copy-start(bf16[384,1152]{1,0:T(8,128)(2,1)} %param.9) | copy-start | bytes 2654212
Sparse Core Ops, SparseCore 0:
  11.7 48.7 all-reduce.2
  63.5 65.3 all-gather.2
where the time goes:
time: 156 us
  waiting for transfers between devices  99.4 us (64%)
  blocking collectives  23.8 us (15%)
  between operations  16.2 us (10%)
  matrix products  9.9 us (6%)
  other arithmetic  4.2 us (3%)
  local copies, waits for them, and re-layouts  2.31 us (1%)
    all_gather x1, waiting for transfers between devices, per_device(): visit_rows = lax.all_gather(counterpart_slice, 'blk', axis=0, tiled=True)  50.5 us
    psum x1, waiting for transfers between devices, per_device(): both_sums = lax.psum(stacked, ('sec', 'mp'))  48.8 us
    unnamed x1, blocking collectives  12.1 us
    all_gather x1, blocking collectives, per_device(): both_grads = lax.all_gather(own_demb[None], 'sec', axis=0, tiled=True)  11.7 us
    dot_general x1, matrix products, per_device(): lax.dot_general(resident_slice, visit_rows, (((1,), (1,)), ((), ())), pre...  4.68 us
  transfers between devices with their start and end apart: 2, of which 2 were waited for; matrix products, arithmetic and copies ran while one was open for 1% of the time, Pallas kernels for 0%

commit v1 on v0

--- a/solution.py
+++ b/solution.py
@@ -31,7 +31,32 @@
     counterpart_slice = other_unit.astype(jnp.bfloat16)
     sharpness_factor = jnp.exp(natural_log_multiplier[0])
     shift_quantity = logit_bias[0]
-    visit_rows = lax.all_gather(counterpart_slice, "blk", axis=0, tiled=True)
+    opened, passed, field_out = (
+        jax.lax.axis_size("blk"),
+        jax.lax.axis_index("blk"),
+        counterpart_slice.shape[0],
+    )
+    seen = [(pp, (pp + 1) % opened) for pp in range(opened)]
+    visit_rows = jnp.zeros(
+        (*counterpart_slice.shape[:0], opened * field_out, *counterpart_slice.shape[1:]),
+        counterpart_slice.dtype,
+    )
+    visit_rows = lax.dynamic_update_slice_in_dim(
+        visit_rows, counterpart_slice, passed * field_out, axis=0
+    )
+    items = [(pp, (pp - 1) % opened) for pp in range(opened)]
+    answer = opened // 2
+    d_next = fresh = counterpart_slice
+    for rr in [*range(1, answer + 1)]:
+        d_next = jax.lax.ppermute(d_next, "blk", seen)
+        visit_rows = lax.dynamic_update_slice_in_dim(
+            visit_rows, d_next, (passed - rr) % opened * field_out, axis=0
+        )
+        if rr < opened - answer:
+            fresh = jax.lax.ppermute(fresh, "blk", items)
+            visit_rows = lax.dynamic_update_slice_in_dim(
+                visit_rows, fresh, (passed + rr) % opened * field_out, axis=0
+            )
     visited_ids = lax.all_gather(match_cluster_labels, "blk", axis=0, tiled=True)
     agreement_scores_matrix = (
         sharpness_factor

time: 156 us -> 174 us (1.12)
  waiting for transfers between devices: 99.4 us -> 82.2 us
  starting transfers between devices: 0.08 us -> 16.7 us
  local copies, waits for them, and re-layouts: 2.31 us -> 10.9 us
  blocking collectives: 23.8 us -> 31.3 us
  matrix products: 9.9 us -> 11.7 us
    all_gather x1 -> x0, waiting for transfers between devices: 50.5 us -> none  [per_device(): visit_rows = lax.all_gather(counterpart_slice, 'blk', axis=0, tiled=True)]
    ppermute x0 -> x7, waiting for transfers between devices: none -> 33.3 us  [the longest x4 33.3 us: per_device(): d_next = jax.lax.ppermute(d_next, 'blk', seen)]
    ppermute x0 -> x7, starting transfers between devices: none -> 16.7 us  [the longest x3 9.67 us: per_device(): fresh = jax.lax.ppermute(fresh, 'blk', items)]
    unnamed x1, blocking collectives: 12.1 us -> 22.2 us
    dynamic_update_slice x0 -> x7, local copies, waits for them, and re-layouts: none -> 6.66 us  [the longest x4 4.24 us: per_device(): lax.dynamic_update_slice_in_dim(visit_rows, d_next, (passed - rr) % opene...]
    all_gather x1, blocking collectives: 11.7 us -> 9.11 us  [per_device(): both_grads = lax.all_gather(own_demb[None], 'sec', axis=0, tiled=True)]
    broadcast_in_dim x0 -> x1, local copies, waits for them, and re-layouts: none -> 2.01 us  [per_device(): jnp.zeros((*counterpart_slice.shape[:0], opened * field_out, *counterpart...]
    dot_general x1, matrix products: 1.12 us -> 3.12 us  [per_device(): jnp.dot(penalty_factor, visit_rows, preferred_element_type=jnp.float32)]
  transfers between devices with their start and end apart: 2 -> 8, of which waited for: 2 -> 4; matrix products, arithmetic and copies ran while one was open for 1% -> 4% of each run, Pallas kernels for 0% -> 0%
where the time goes in v1:
time: 174 us; the launch traced here: 173 us
  waiting for transfers between devices  82.2 us (47%)
  blocking collectives  31.3 us (18%)
  starting transfers between devices  16.7 us (10%)
  between operations  16.2 us (9%)
  matrix products  11.7 us (7%)
  local copies, waits for them, and re-layouts  10.9 us (6%)
  other arithmetic  4.28 us (2%)
    psum x1, waiting for transfers between devices, per_device(): both_sums = lax.psum(stacked, ('sec', 'mp'))  48.9 us
    ppermute x4, waiting for transfers between devices, per_device(): d_next = jax.lax.ppermute(d_next, 'blk', seen)  33.3 us
    unnamed x1, blocking collectives  22.2 us
    ppermute x3, starting transfers between devices, per_device(): fresh = jax.lax.ppermute(fresh, 'blk', items)  9.67 us
    all_gather x1, blocking collectives, per_device(): both_grads = lax.all_gather(own_demb[None], 'sec', axis=0, tiled=True)  9.11 us
    ppermute x4, starting transfers between devices, per_device(): d_next = jax.lax.ppermute(d_next, 'blk', seen)  7.03 us
    dot_general x1, matrix products, per_device(): lax.dot_general(resident_slice, visit_rows, (((1,), (1,)), ((), ())), pre...  4.53 us
    dynamic_update_slice x4, local copies, waits for them, and re-layouts, per_device(): lax.dynamic_update_slice_in_dim(visit_rows, d_next, (passed - rr) % opene...  4.24 us
  transfers between devices with their start and end apart: 8, of which 4 were waited for; matrix products, arithmetic and copies ran while one was open for 4% of the time, Pallas kernels for 0%

profile of v1, /device:TPU:0, one launch (start us, length us, event | category | flops | bytes accessed | tf_op | source)
XLA Modules:
  0.0 173.3 jit_solution(9222464023707049804)
XLA Ops:
  7.2 0.0 copy-start
  7.2 0.0 copy-start.4
  7.2 0.0 copy-start.2
  7.2 0.0 all-reduce.3.cloned.1.call-start
  7.2 1.2 copy-done
  8.4 1.4 convolution_bitcast_fusion
  9.8 0.0 copy-done.4
  9.8 0.0 copy-done.2
  9.8 0.4 convolution_bitcast_fusion.1
  10.2 1.4 pad_maximum_fusion
  11.6 0.0 all-reduce.3.cloned.1.call-update
  11.6 48.9 %all-reduce.3.cloned.1.call-done = f32[2,192,1152]{2,1,0:T(8,128)} async-done(((f32[2,192,1152]{2,1,0:T(8,128)}), f32[2,192,1152]{2,1,0:T(8,128)}) %all-reduce.3.cloned.1.call-update) | async-done | bytes 1769488 | tf_op jit(solution)/shard_map/psum | solution.py:25
  60.5 1.6 fusion.7
  62.2 0.0 copy-start.1
  62.2 2.0 %broadcast_in_dim.24 = bf16[1536,1152]{1,0:T(8,128)(2,1)} broadcast(bf16[]{:T(256)} %constant.75.clone.1), dimensions={} | broadcast | bytes 3538946 | tf_op jit(solution)/shard_map/broadcast_in_dim | solution.py:40
  64.2 0.1 copy-done.1
  64.3 1.1 constant_dynamic-update-slice_fusion.7
  65.3 1.5 collective-permute-start
  66.8 3.2 %collective-permute-start.1 = (bf16[192,1152]{1,0:T(8,128)(2,1)}, bf16[192,1152]{1,0:T(8,128)(2,1)S(1)}, u32[]{:S(2)}, u32[]{:S(2)}) collective-permute-start(bf16[192,1152]{1,0:T(8,128)(2,1)} %get-tuple-element.6), channel_id=1, source_target_pairs={{0,14},{2,0},{4,2},{6,4},{8,6},{10,8},{12,10},{14,12},{1,15},{3,1}... | collective-permute-start | bytes 1327112 | tf_op jit(solution)/shard_map/ppermute | solution.py:56
  71.4 0.6 dynamic-slice
  72.7 0.3 dynamic-update-slice
  73.0 22.2 %all-reduce = s32[1536]{0:T(1024)S(1)} all-reduce(s32[1536]{0:T(1024)S(1)} %dynamic-update-slice), channel_id=1, replica_groups=mesh['sec'=2,'blk'=8,'mp'=2] {'blk'}, use_global_device_ids=true, to_apply=%add | all-reduce | flops 1536 | bytes 12288
  95.2 0.0 collective-permute-done
  95.2 0.7 collective-permute-start.2
  95.9 0.0 collective-permute-done.1
  95.9 4.1 %collective-permute-start.3 = (bf16[192,1152]{1,0:T(8,128)(2,1)S(1)}, bf16[192,1152]{1,0:T(8,128)(2,1)S(1)}, u32[]{:S(2)}, u32[]{:S(2)}) collective-permute-start(bf16[192,1152]{1,0:T(8,128)(2,1)S(1)} %collective-permute-done.1), channel_id=1, source_target_pairs={{0,14},{2,0},{4,2},{6,4},{8,6},{10,8},{12,10},{14,12},{1,15},{3,1}... | collective-permute-start | bytes 1327112 | tf_op jit(solution)/shard_map/ppermute | solution.py:56
  100.0 1.8 %constant_dynamic-update-slice_fusion.6 = bf16[1536,1152]{1,0:T(8,128)(2,1)} fusion(bf16[1536,1152]{1,0:T(8,128)(2,1)} %get-tuple-element.5, bf16[192,1152]{1,0:T(8,128)(2,1)} %collective-permute-done, s32[]{:T(128)S(6)} %select_n.75), kind=kLoop, calls=%fused_computation.38 | loop fusion | bytes 884740 | tf_op jit(solution)/shard_map/dynamic_update_slice | solution.py:52
  101.8 0.8 constant_dynamic-update-slice_fusion.5
  102.6 10.6 %collective-permute-done.2 = bf16[192,1152]{1,0:T(8,128)(2,1)S(1)} collective-permute-done((bf16[192,1152]{1,0:T(8,128)(2,1)}, bf16[192,1152]{1,0:T(8,128)(2,1)S(1)}, u32[]{:S(2)}, u32[]{:S(2)}) %collective-permute-start.2) | collective-permute-done | bytes 442400 | tf_op jit(solution)/shard_map/ppermute | solution.py:51
  113.2 2.4 %collective-permute-start.4 = (bf16[192,1152]{1,0:T(8,128)(2,1)S(1)}, bf16[192,1152]{1,0:T(8,128)(2,1)S(1)}, u32[]{:S(2)}, u32[]{:S(2)}) collective-permute-start(bf16[192,1152]{1,0:T(8,128)(2,1)S(1)} %collective-permute-done.2), channel_id=1, source_target_pairs={{0,2},{2,4},{4,6},{6,8},{8,10},{10,12},{12,14},{14,0},{1,3},{3,5},... | collective-permute-start | bytes 1327112 | tf_op jit(solution)/shard_map/ppermute | solution.py:51
  115.6 0.0 collective-permute-done.3
  115.6 2.3 %collective-permute-start.5 = (bf16[192,1152]{1,0:T(8,128)(2,1)S(1)}, bf16[192,1152]{1,0:T(8,128)(2,1)S(1)}, u32[]{:S(2)}, u32[]{:S(2)}) collective-permute-start(bf16[192,1152]{1,0:T(8,128)(2,1)S(1)} %collective-permute-done.3), channel_id=1, source_target_pairs={{0,14},{2,0},{4,2},{6,4},{8,6},{10,8},{12,10},{14,12},{1,15},{3,1}... | collective-permute-start | bytes 1327112 | tf_op jit(solution)/shard_map/ppermute | solution.py:56
  117.9 0.8 constant_dynamic-update-slice_fusion.4
  118.8 0.8 constant_dynamic-update-slice_fusion.3
  119.6 13.0 %collective-permute-done.4 = bf16[192,1152]{1,0:T(8,128)(2,1)S(1)} collective-permute-done((bf16[192,1152]{1,0:T(8,128)(2,1)S(1)}, bf16[192,1152]{1,0:T(8,128)(2,1)S(1)}, u32[]{:S(2)}, u32[]{:S(2)}) %collective-permute-start.4) | collective-permute-done | bytes 442400 | tf_op jit(solution)/shard_map/ppermute | solution.py:51
  132.5 2.5 %collective-permute-start.6 = (bf16[192,1152]{1,0:T(8,128)(2,1)S(1)}, bf16[192,1152]{1,0:T(8,128)(2,1)S(1)}, u32[]{:S(2)}, u32[]{:S(2)}) collective-permute-start(bf16[192,1152]{1,0:T(8,128)(2,1)S(1)} %collective-permute-done.4), channel_id=1, source_target_pairs={{0,2},{2,4},{4,6},{6,8},{8,10},{10,12},{12,14},{14,0},{1,3},{3,5},... | collective-permute-start | bytes 1327112 | tf_op jit(solution)/shard_map/ppermute | solution.py:51
  135.0 0.8 constant_dynamic-update-slice_fusion.2
  135.8 0.0 collective-permute-done.5
  135.8 0.8 constant_dynamic-update-slice_fusion.1
  136.6 9.7 %collective-permute-done.6 = bf16[192,1152]{1,0:T(8,128)(2,1)S(1)} collective-permute-done((bf16[192,1152]{1,0:T(8,128)(2,1)S(1)}, bf16[192,1152]{1,0:T(8,128)(2,1)S(1)}, u32[]{:S(2)}, u32[]{:S(2)}) %collective-permute-start.6) | collective-permute-done | bytes 442400 | tf_op jit(solution)/shard_map/ppermute | solution.py:51
  146.3 0.8 constant_dynamic-update-slice_fusion
  147.1 4.5 %fusion.4 = (f32[192]{0:T(256)}, f32[192,1536]{1,0:T(8,128)S(1)}) fusion(f32[]{:T(128)} %bitcast.38, bf16[1536,1152]{1,0:T(8,128)(2,1)} %constant_dynamic-update-slice_fusion, f32[192]{0:T(256)S(1)} %add_sqrt_fusion.1, f32[2,192,1152]{2,1,0:T(8,128)S(1)} %copy-done.1, s32[]{:T(128)S(6)} %select_n.71, f32[]{:T(128)} %bitcast.1, s32[1536]{0:T(1024)S(1)} %all-reduce, ...), kind=kOutput, calls=%fused_computation.11 | convolution fusion | flops 683753280 | bytes 5614348 | tf_op jit(solution)/shard_map/dot_general | solution.py:63
  151.7 3.1 %multiply_reduce_fusion = (f32[192]{0:T(256)S(1)}, f32[192,1152]{1,0:T(8,128)S(1)}) fusion(f32[192]{0:T(256)S(1)} %add_sqrt_fusion.1, f32[2,192,1152]{2,1,0:T(8,128)S(1)} %copy-done.1, s32[]{:T(128)S(6)} %select_n.71, bf16[1536,1152]{1,0:T(8,128)(2,1)} %constant_dynamic-update-slice_fusion, f32[192,1536]{1,0:T(8,128)S(1)} %get-tuple-element.8, ...), kind=kOutput, calls=%fused_computation.22 | convolution fusion | flops 682499904 | bytes 6496520 | tf_op jit(solution)/shard_map/dot_general | solution.py:77
  154.8 0.2 divide_convert_fusion
  155.0 0.0 copy-start.3
  155.0 9.1 %all-gather = bf16[384,1152]{1,0:T(8,128)(2,1)S(1)} all-gather(bf16[192,1152]{1,0:T(8,128)(2,1)S(1)} %divide_convert_fusion), channel_id=2, replica_groups=mesh['sec'=2,'blk'=8,'mp'=2] {'sec'}, dimensions={0}, use_global_device_ids=true | all-gather | bytes 1327104 | tf_op jit(solution)/shard_map/all_gather | solution.py:81
  164.1 1.2 convolution_convert_fusion
  165.4 1.1 convolution_convert_fusion.1
  (8 shorter events, 0.0 us)
Async XLA Ops:
  7.2 1.3 copy-start
  7.2 2.6 %copy-start.4 = (bf16[192,384]{1,0:T(8,128)(2,1)S(1)}, bf16[192,384]{1,0:T(8,128)(2,1)}, u32[]{:S(2)}) copy-start(bf16[192,384]{1,0:T(8,128)(2,1)} %param.7) | copy-start | bytes 442372
  7.2 2.6 %copy-start.2 = (bf16[384,1152]{1,0:T(8,128)(2,1)S(1)}, bf16[384,1152]{1,0:T(8,128)(2,1)}, u32[]{:S(2)}) copy-start(bf16[384,1152]{1,0:T(8,128)(2,1)} %param.9) | copy-start | bytes 2654212
  7.2 53.3 %all-reduce.3.cloned.1.call-start = ((), (), s32[]{:S(2)}) async-start(), calls=%async_computation | async-start | bytes 3538944 | tf_op jit(solution)/shard_map/psum | solution.py:25
  62.2 2.1 %copy-start.1 = (f32[2,192,1152]{2,1,0:T(8,128)S(1)}, f32[2,192,1152]{2,1,0:T(8,128)}, u32[]{:S(2)}) copy-start(f32[2,192,1152]{2,1,0:T(8,128)} %all-reduce.3.cloned.1.call-done) | copy-start | bytes 5308420
  64.3 7.1 %copy-start.6 = (u32[32]{0:T(128)S(1)}, u32[32]{0:T(128)}, u32[]{:S(2)}) copy-start(u32[32]{0:T(128)} %constant.89) | copy-start | bytes 388
  64.3 8.4 %copy-start.5 = (s32[192]{0:T(256)S(1)}, s32[192]{0:T(256)}, u32[]{:S(2)}) copy-start(s32[192]{0:T(256)} %param.13) | copy-start | bytes 2308
  65.3 29.9 %collective-permute-start = (bf16[192,1152]{1,0:T(8,128)(2,1)}, bf16[192,1152]{1,0:T(8,128)(2,1)}, u32[]{:S(2)}, u32[]{:S(2)}) collective-permute-start(bf16[192,1152]{1,0:T(8,128)(2,1)} %get-tuple-element.6), channel_id=1, source_target_pairs={{0,2},{2,4},{4,6},{6,8},{8,10},{10,12},{12,14},{14,0},{1,3},{3,5},... | collective-permute-start | bytes 1327112 | tf_op jit(solution)/shard_map/ppermute | solution.py:51
  66.8 29.1 %collective-permute-start.1 = (bf16[192,1152]{1,0:T(8,128)(2,1)}, bf16[192,1152]{1,0:T(8,128)(2,1)S(1)}, u32[]{:S(2)}, u32[]{:S(2)}) collective-permute-start(bf16[192,1152]{1,0:T(8,128)(2,1)} %get-tuple-element.6), channel_id=1, source_target_pairs={{0,14},{2,0},{4,2},{6,4},{8,6},{10,8},{12,10},{14,12},{1,15},{3,1}... | collective-permute-start | bytes 1327112 | tf_op jit(solution)/shard_map/ppermute | solution.py:56
  95.2 18.0 %collective-permute-start.2 = (bf16[192,1152]{1,0:T(8,128)(2,1)}, bf16[192,1152]{1,0:T(8,128)(2,1)S(1)}, u32[]{:S(2)}, u32[]{:S(2)}) collective-permute-start(bf16[192,1152]{1,0:T(8,128)(2,1)} %collective-permute-done), channel_id=1, source_target_pairs={{0,2},{2,4},{4,6},{6,8},{8,10},{10,12},{12,14},{14,0},{1,3},{3,5},... | collective-permute-start | bytes 1327112 | tf_op jit(solution)/shard_map/ppermute | solution.py:51
  95.9 19.7 %collective-permute-start.3 = (bf16[192,1152]{1,0:T(8,128)(2,1)S(1)}, bf16[192,1152]{1,0:T(8,128)(2,1)S(1)}, u32[]{:S(2)}, u32[]{:S(2)}) collective-permute-start(bf16[192,1152]{1,0:T(8,128)(2,1)S(1)} %collective-permute-done.1), channel_id=1, source_target_pairs={{0,14},{2,0},{4,2},{6,4},{8,6},{10,8},{12,10},{14,12},{1,15},{3,1}... | collective-permute-start | bytes 1327112 | tf_op jit(solution)/shard_map/ppermute | solution.py:56
  113.2 19.3 %collective-permute-start.4 = (bf16[192,1152]{1,0:T(8,128)(2,1)S(1)}, bf16[192,1152]{1,0:T(8,128)(2,1)S(1)}, u32[]{:S(2)}, u32[]{:S(2)}) collective-permute-start(bf16[192,1152]{1,0:T(8,128)(2,1)S(1)} %collective-permute-done.2), channel_id=1, source_target_pairs={{0,2},{2,4},{4,6},{6,8},{8,10},{10,12},{12,14},{14,0},{1,3},{3,5},... | collective-permute-start | bytes 1327112 | tf_op jit(solution)/shard_map/ppermute | solution.py:51
  115.6 20.2 %collective-permute-start.5 = (bf16[192,1152]{1,0:T(8,128)(2,1)S(1)}, bf16[192,1152]{1,0:T(8,128)(2,1)S(1)}, u32[]{:S(2)}, u32[]{:S(2)}) collective-permute-start(bf16[192,1152]{1,0:T(8,128)(2,1)S(1)} %collective-permute-done.3), channel_id=1, source_target_pairs={{0,14},{2,0},{4,2},{6,4},{8,6},{10,8},{12,10},{14,12},{1,15},{3,1}... | collective-permute-start | bytes 1327112 | tf_op jit(solution)/shard_map/ppermute | solution.py:56
  132.5 13.8 %collective-permute-start.6 = (bf16[192,1152]{1,0:T(8,128)(2,1)S(1)}, bf16[192,1152]{1,0:T(8,128)(2,1)S(1)}, u32[]{:S(2)}, u32[]{:S(2)}) collective-permute-start(bf16[192,1152]{1,0:T(8,128)(2,1)S(1)} %collective-permute-done.4), channel_id=1, source_target_pairs={{0,2},{2,4},{4,6},{6,8},{8,10},{10,12},{12,14},{14,0},{1,3},{3,5},... | collective-permute-start | bytes 1327112 | tf_op jit(solution)/shard_map/ppermute | solution.py:51
  155.0 10.4 %copy-start.3 = (bf16[384,1152]{1,0:T(8,128)(2,1)S(1)}, bf16[384,1152]{1,0:T(8,128)(2,1)}, u32[]{:S(2)}) copy-start(bf16[384,1152]{1,0:T(8,128)(2,1)} %param.9) | copy-start | bytes 2654212
Sparse Core Ops, SparseCore 0:
  11.7 48.7 all-reduce.2
